TPU v7x, 256 devices: a whole 4x4x8 slice. The times are simulated.
256 devices in a mesh: group: 8 (over x, core), expert: 32 (over y, z).
Axes of the slice: x: 4, y: 4, z: 8, core: 2. Of those that a mesh axis runs over, the one named last changes fastest.
Arguments:
- resid: bfloat16 [32768, 2048], P(('group', 'expert')), may hold values from -6 to 6
- queries: bfloat16 [32768, 2048], P(('group', 'expert')), may hold values from -48 to 48
- span_kv: bfloat16 [2, 32768, 2048], P(None, ('group', 'expert')), may hold values from -4 to 4
- cache_kv: bfloat16 [2, 256, 2, 128, 2048], P(None, ('group', 'expert')), may hold values from -6 to 6
- seg_len: int32 [256, 2], P(('group', 'expert')), may hold values from 0 to 128, as said below
- o_rows: bfloat16 [2048, 2048], P('expert'), may hold values from -0.125 to 0.125
- norm_gain: float32 [2048], replicated, may hold values from 0.25 to 1.75
- routes: int32 [32768, 8], P(('group', 'expert')), may hold values from 0 to 31, all different within a row; in each aligned block of 128 rows (0 to 127, 128 to 255, ...) at most 48 rows name the same one
- route_wts: float32 [32768, 8], P(('group', 'expert')), may hold values from 0.05 to 0.6
- w_in: bfloat16 [32, 2048, 1024], P('expert'), may hold values from -0.125 to 0.125
- w_out: bfloat16 [32, 512, 2048], P('expert'), may hold values from -0.25 to 0.25
Outputs:
- layer_out: bfloat16 [32768, 2048], P(('group', 'expert'))
Inputs may be any that keep to these rules, and one draw needn't show every extreme that they name: seg_len[d, 0] is 1 to 128; seg_len[d, 1] is 0 (the paired request is short) or 1 to 128; seg_len[0, 0] and seg_len[0, 1] are 128 and seg_len[1, 1] is 0. `routes`: each row names 8 different experts; among the 128 rows of one device no expert is named more than 48 times.
All inputs are finite; a program needn't handle non-finite values.
Results may differ from a plain program's by a relative error of at most 0.0053.
Values may be sent and summed in bfloat16 or wider, within the bound.
A program may use at most 128 MiB of HBM per device.

v0:
```python
import math

import jax
import jax.numpy as jnp
from jax import lax
from jax.sharding import PartitionSpec as P

HEADS = 16
HD = 128
FF = 512
TOPK = 8


def swapped(block, axis, distance):
    count = lax.axis_size(axis)
    route = []
    for low in range(count):
        high = low | 1 << distance
        if high != low and high < count:
            route += [(low, high), (high, low)]
    return lax.ppermute(block, axis, route)


def attend(query_rows, key_rows, value_rows, valid_keys):
    q_heads = query_rows.reshape(query_rows.shape[0], HEADS, HD)
    k_heads = key_rows.reshape(key_rows.shape[0], HEADS, HD)
    v_heads = value_rows.reshape(value_rows.shape[0], HEADS, HD)
    scores = jnp.einsum("chd,shd->hcs", q_heads, k_heads, preferred_element_type=jnp.float32) * (
        1.0 / math.sqrt(HD)
    )
    scores = jnp.where(valid_keys[None, None, :], scores, -1e30)
    peak_score = jnp.max(scores, axis=-1)
    expo = jnp.where(valid_keys[None, None, :], jnp.exp(scores - peak_score[..., None]), 0.0)
    totals = jnp.sum(expo, axis=-1)
    probs_low = expo.astype(jnp.bfloat16)
    accum_out = jnp.einsum("hcs,shd->chd", probs_low, v_heads, preferred_element_type=jnp.float32)
    return (peak_score, totals, accum_out)


def merge_parts(first, second):
    peak_a, total_a, accum_a = first
    peak_b, total_b, accum_b = second
    peak_both = jnp.maximum(peak_a, peak_b)
    scale_a = jnp.exp(peak_a - peak_both).T
    scale_b = jnp.exp(peak_b - peak_both).T
    numer = accum_a * scale_a[:, :, None] + accum_b * scale_b[:, :, None]
    denom = total_a.T * scale_a + total_b.T * scale_b
    merged = numer / denom[:, :, None]
    return merged.reshape(merged.shape[0], -1).astype(jnp.bfloat16)


def expert_mlp(token_rows, weight_in, weight_out):
    joined = jnp.dot(token_rows, weight_in, preferred_element_type=jnp.float32)
    hidden = (jax.nn.silu(joined[:, :FF]) * joined[:, FF:]).astype(jnp.bfloat16)
    return jnp.dot(hidden, weight_out, preferred_element_type=jnp.float32).astype(jnp.bfloat16)


def shards(
    resid, queries, span_kv, cache_kv, seg_len, o_rows, norm_gain, routes, route_wts, w_in, w_out
):
    span_rows = queries.shape[0]
    seg_rows = cache_kv.shape[3]
    width = queries.shape[1]
    experts_here = lax.axis_size("expert")
    positions = jnp.arange(seg_rows, dtype=jnp.int32)
    keys_a = jnp.concatenate([span_kv[0], cache_kv[0, 0, 0]], axis=0)
    vals_a = jnp.concatenate([span_kv[1], cache_kv[1, 0, 0]], axis=0)
    valid_a = jnp.concatenate([jnp.ones((span_rows,), bool), positions < seg_len[0, 0]])
    part_a = attend(queries, keys_a, vals_a, valid_a)
    length_low = seg_len[0, 1:2].astype(jnp.float32).astype(jnp.bfloat16)
    fetched, fetched_len = swapped((cache_kv[:, 0, 1], length_low), "group", 0)
    valid_b = positions.astype(jnp.float32) < fetched_len[0].astype(jnp.float32)
    part_b = attend(queries, fetched[0], fetched[1], valid_b)
    attended = merge_parts(part_a, part_b)
    projected = jnp.dot(
        attended,
        lax.all_gather(o_rows, "expert", axis=0, tiled=True),
        preferred_element_type=jnp.float32,
    )
    residual = resid.astype(jnp.float32) + projected
    normed = (
        residual
        * lax.rsqrt(jnp.mean(residual * residual, axis=-1, keepdims=True) + 1e-05)
        * norm_gain
    ).astype(jnp.bfloat16)
    capacity = min(span_rows, span_rows * TOPK * 3 // (2 * experts_here))
    onehot = (
        routes[:, :, None] == jnp.arange(experts_here, dtype=jnp.int32)[None, None, :]
    ).astype(jnp.int32)
    counts = jnp.sum(onehot, axis=1)
    before = jnp.cumsum(counts, axis=0) - counts
    slot_ids = jnp.sum(onehot * before[:, None, :], axis=-1)
    flat_slot = routes * capacity + slot_ids
    placing = jnp.any(
        flat_slot[None, :, :]
        == jnp.arange(experts_here * capacity, dtype=jnp.int32)[:, None, None],
        axis=-1,
    )
    outgoing = jnp.dot(
        placing.astype(jnp.bfloat16), normed, preferred_element_type=jnp.float32
    ).astype(jnp.bfloat16)
    outgoing = outgoing.reshape(experts_here, capacity, width)
    arrived = lax.all_to_all(outgoing, "expert", split_axis=0, concat_axis=0, tiled=True)
    flat_rows = arrived.reshape(-1, width)
    output_rows = expert_mlp(flat_rows, w_in[0], w_out[0]).reshape(arrived.shape)
    returned_rows = lax.all_to_all(output_rows, "expert", split_axis=0, concat_axis=0, tiled=True)
    returned_rows = returned_rows.reshape(experts_here * capacity, width)
    expert_sum = jnp.zeros((span_rows, width), jnp.float32)
    for route_k in range(TOPK):
        picked = returned_rows[flat_slot[:, route_k]].astype(jnp.float32)
        expert_sum = expert_sum + route_wts[:, route_k, None] * picked
    return (residual + expert_sum).astype(jnp.bfloat16)


def solution(mesh):
    placed = (
        P(("group", "expert"), None),
        P(("group", "expert"), None),
        P(None, ("group", "expert"), None),
        P(None, ("group", "expert"), None, None, None),
        P(("group", "expert"), None),
        P("expert", None),
        P(),
        P(("group", "expert"), None),
        P(("group", "expert"), None),
        P("expert", None, None),
        P("expert", None, None),
    )
    return jax.shard_map(
        shards, mesh=mesh, in_specs=placed, out_specs=P(("group", "expert"), None), check_vma=False
    )
```

profile of v0, /device:TPU:33, one launch (start us, length us, event | category | flops | bytes accessed | tf_op | source)
XLA Modules:
  0.0 479.4 jit_solution(5816244615594503621)
XLA Ops:
  7.3 1.3 fusion.66
  9.2 1.6 collective-permute-start
  10.8 1.3 slice.87
  12.1 1.3 copy.55
  13.4 2.1 fusion.65
  15.5 1.3 copy.53
  16.8 1.1 copy.39
  17.9 2.3 fusion.63
  20.2 1.3 copy.54
  23.6 2.1 copy.36
  26.8 5.6 %fusion = pred[1536,128]{1,0:T(8,128)(4,1)S(1)} fusion(s32[128,8]{0,1:T(8,128)S(1)} %multiply_add_fusion), kind=kLoop, calls=%fused_computation.11 | loop fusion | flops 2949120 | bytes 200704 | tf_op jit(solution)/shard_map/reduce_or | solution.py:94
  32.4 1.9 bitcast_reduce_fusion
  34.2 1.3 copy-done.1
  37.0 1.4 fusion.64
  40.0 1.2 fusion.16
  41.2 67.1 %all-gather.2.cloned.1.call-done = bf16[2048,2048]{1,0:T(8,128)(2,1)} async-done(((bf16[64,2048]{1,0:T(8,128)(2,1)}), bf16[2048,2048]{1,0:T(8,128)(2,1)}) %all-gather.2.cloned.1.call-update) | async-done | bytes 8388624 | tf_op jit(solution)/shard_map/all_gather | solution.py:77
  108.3 4.9 %multiply_reduce_fusion = (f32[128]{0:T(128)S(1)}, f32[128,2048]{1,0:T(8,128)S(1)}) fusion(bf16[128,2048]{0,1:T(8,128)(2,1)} %bitcast.126, bf16[2048,2048]{1,0:T(8,128)(2,1)} %all-gather.2.cloned.1.call-done, bf16[128,2048]{1,0:T(8,128)(2,1)} %param.11), kind=kOutput, calls=%fused_computation.44 | convolution fusion | flops 1074790272 | bytes 10486272 | tf_op jit(solution)/shard_map/dot_general | solution.py:75
  113.2 1.9 convolution_convert_fusion.1
  115.1 145.8 %all_to_all.10 = bf16[32,48,2048]{2,1,0:T(8,128)(2,1)S(1)} all-to-all(bf16[32,48,2048]{2,1,0:T(8,128)(2,1)S(1)} %bitcast.120), channel_id=1, replica_groups=mesh['group'=8,'expert'=32] {'expert'}, dimensions={0} | all-to-all | bytes 12582912 | tf_op jit(solution)/shard_map/all_to_all | solution.py:103
  260.9 6.8 %fusion.1 = f32[1536,1024]{1,0:T(8,128)S(1)} fusion(bf16[1536,2048]{1,0:T(8,128)(2,1)S(1)} %bitcast.122, bf16[1,2048,1024]{2,1,0:T(8,128)(2,1)S(1)} %copy-done.9), kind=kOutput, calls=%fused_computation.12 | convolution fusion | flops 6442450944 | bytes 16777216 | tf_op jit(solution)/shard_map/dot_general | solution.py:53
  267.7 5.4 %convolution_convert_fusion = bf16[1536,2048]{1,0:T(8,128)(2,1)} fusion(bf16[1,512,2048]{2,1,0:T(8,128)(2,1)S(1)} %copy-done, f32[1536,1024]{1,0:T(8,128)S(1)} %fusion.1), kind=kOutput, calls=%fused_computation.8 | convolution fusion | flops 3229089792 | bytes 14680064 | tf_op jit(solution)/shard_map/dot_general | solution.py:55
  273.1 7.4 %all-to-all-start.1 = ((bf16[32,48,2048]{2,1,0:T(8,128)(2,1)}), bf16[32,48,2048]{2,1,0:T(8,128)(2,1)}, u32[]{:S(2)}, u32[]{:S(2)}) async-start(bf16[32,48,2048]{2,1,0:T(8,128)(2,1)} %bitcast.121), calls=%async_computation.1 | async-start | bytes 12582912 | tf_op jit(solution)/shard_map/all_to_all | solution.py:106
  280.6 140.9 %all-to-all-done.1 = bf16[32,48,2048]{2,1,0:T(8,128)(2,1)} async-done(((bf16[32,48,2048]{2,1,0:T(8,128)(2,1)}), bf16[32,48,2048]{2,1,0:T(8,128)(2,1)}, u32[]{:S(2)}, u32[]{:S(2)}) %all-to-all-start.1) | async-done | bytes 6291488 | tf_op jit(solution)/shard_map/all_to_all | solution.py:106
  421.5 5.8 %gather_fusion = bf16[128,2048]{1,0:T(8,128)(2,1)} fusion(bf16[1536,2048]{1,0:T(8,128)(2,1)} %bitcast.24, s32[1024]{0:T(1024)S(1)} %get-tuple-element.45), kind=kCustom, calls=%fused_computation | custom fusion | bytes 1049088 | tf_op jit(solution)/shard_map/gather | solution.py:110
  427.3 5.9 %gather_fusion.1 = bf16[128,2048]{1,0:T(8,128)(2,1)} fusion(bf16[1536,2048]{1,0:T(8,128)(2,1)} %bitcast.24, s32[1024]{0:T(1024)S(1)} %get-tuple-element.44), kind=kCustom, calls=%fused_computation.1 | custom fusion | bytes 1049088 | tf_op jit(solution)/shard_map/gather | solution.py:110
  433.2 5.9 %gather_fusion.2 = bf16[128,2048]{1,0:T(8,128)(2,1)} fusion(bf16[1536,2048]{1,0:T(8,128)(2,1)} %bitcast.24, s32[1024]{0:T(1024)S(1)} %get-tuple-element.43), kind=kCustom, calls=%fused_computation.2 | custom fusion | bytes 1049088 | tf_op jit(solution)/shard_map/gather | solution.py:110
  439.1 5.9 %gather_fusion.3 = bf16[128,2048]{1,0:T(8,128)(2,1)} fusion(bf16[1536,2048]{1,0:T(8,128)(2,1)} %bitcast.24, s32[1024]{0:T(1024)S(1)} %get-tuple-element.42), kind=kCustom, calls=%fused_computation.3 | custom fusion | bytes 1049088 | tf_op jit(solution)/shard_map/gather | solution.py:110
  444.9 5.8 %gather_fusion.4 = bf16[128,2048]{1,0:T(8,128)(2,1)} fusion(bf16[1536,2048]{1,0:T(8,128)(2,1)} %bitcast.24, s32[1024]{0:T(1024)S(1)} %get-tuple-element.41), kind=kCustom, calls=%fused_computation.4 | custom fusion | bytes 1049088 | tf_op jit(solution)/shard_map/gather | solution.py:110
  450.7 5.8 %gather_fusion.5 = bf16[128,2048]{1,0:T(8,128)(2,1)} fusion(bf16[1536,2048]{1,0:T(8,128)(2,1)} %bitcast.24, s32[1024]{0:T(1024)S(1)} %get-tuple-element.40), kind=kCustom, calls=%fused_computation.5 | custom fusion | bytes 1049088 | tf_op jit(solution)/shard_map/gather | solution.py:110
  456.6 6.1 %gather_fusion.6 = bf16[128,2048]{1,0:T(8,128)(2,1)} fusion(bf16[1536,2048]{1,0:T(8,128)(2,1)} %bitcast.24, s32[1024]{0:T(1024)S(1)} %get-tuple-element.39), kind=kCustom, calls=%fused_computation.6 | custom fusion | bytes 1049088 | tf_op jit(solution)/shard_map/gather | solution.py:110
  462.6 5.8 %gather_fusion.7 = bf16[128,2048]{1,0:T(8,128)(2,1)} fusion(bf16[1536,2048]{1,0:T(8,128)(2,1)} %bitcast.24, s32[1024]{0:T(1024)S(1)} %get-tuple-element.38), kind=kCustom, calls=%fused_computation.7 | custom fusion | bytes 1049088 | tf_op jit(solution)/shard_map/gather | solution.py:110
  468.5 3.9 add_convert_fusion
  (48 shorter events, 6.1 us)
Async XLA Ops:
  6.5 261.2 %copy-start = (bf16[1,512,2048]{2,1,0:T(8,128)(2,1)S(1)}, bf16[1,512,2048]{2,1,0:T(8,128)(2,1)}, u32[]{:S(2)}) copy-start(bf16[1,512,2048]{2,1,0:T(8,128)(2,1)} %param.21) | copy-start | bytes 6291460
  6.5 101.7 %all-gather.2.cloned.1.call-start = ((), (), s32[]{:S(2)}) async-start(), calls=%async_computation.2 | async-start | bytes 8650752 | tf_op jit(solution)/shard_map/all_gather | solution.py:77
  9.2 27.0 %collective-permute-start = (bf16[1]{0:T(256)(128)(2,1)}, bf16[1]{0:T(256)(128)(2,1)}, u32[]{:S(2)}, u32[]{:S(2)}) collective-permute-start(bf16[1]{0:T(256)(128)(2,1)} %bitcast.8), channel_id=1, source_target_pairs={{0,32},{32,0},{64,96},{96,64},{128,160},{160,128},{192,224},{224,1... | collective-permute-start | bytes 14 | tf_op jit(solution)/shard_map/ppermute | solution.py:21
  13.4 23.5 %collective-permute-start.1 = (bf16[2,128,2048]{1,2,0:T(8,128)(2,1)}, bf16[2,128,2048]{1,2,0:T(8,128)(2,1)}, u32[]{:S(2)}, u32[]{:S(2)}) collective-permute-start(bf16[2,128,2048]{1,2,0:T(8,128)(2,1)} %bitcast.127), channel_id=1, source_target_pairs={{0,32},{32,0},{64,96},{96,64},{128,160},{160,128},{192,224},{224,1... | collective-permute-start | bytes 3145736 | tf_op jit(solution)/shard_map/ppermute | solution.py:21
  17.9 7.8 %copy-start.6 = (s32[128,8]{0,1:T(8,128)S(1)}, s32[128,8]{0,1:T(8,128)}, u32[]{:S(2)}) copy-start(s32[128,8]{0,1:T(8,128)} %param.18) | copy-start | bytes 12292
  34.2 1.4 copy-start.1
  34.2 4.2 copy-start.3
  36.2 3.0 copy-start.4
  36.9 2.3 copy-start.2
  36.9 2.3 copy-start.5
  108.3 5.0 %copy-start.7 = (f32[2048]{0:T(1024)S(1)}, f32[2048]{0:T(1024)}, u32[]{:S(2)}) copy-start(f32[2048]{0:T(1024)} %param.17) | copy-start | bytes 24580
  115.1 145.8 %copy-start.9 = (bf16[1,2048,1024]{2,1,0:T(8,128)(2,1)S(1)}, bf16[1,2048,1024]{2,1,0:T(8,128)(2,1)}, u32[]{:S(2)}) copy-start(bf16[1,2048,1024]{2,1,0:T(8,128)(2,1)} %param.20) | copy-start | bytes 12582916
  273.1 7.4 %copy-start.8 = (f32[128,8]{0,1:T(8,128)S(1)}, f32[128,8]{0,1:T(8,128)}, u32[]{:S(2)}) copy-start(f32[128,8]{0,1:T(8,128)} %param.19) | copy-start | bytes 12292
  273.1 148.4 %all-to-all-start.1 = ((bf16[32,48,2048]{2,1,0:T(8,128)(2,1)}), bf16[32,48,2048]{2,1,0:T(8,128)(2,1)}, u32[]{:S(2)}, u32[]{:S(2)}) async-start(bf16[32,48,2048]{2,1,0:T(8,128)(2,1)} %bitcast.121), calls=%async_computation.1 | async-start | bytes 12582912 | tf_op jit(solution)/shard_map/all_to_all | solution.py:106
Sparse Core Ops, SparseCore 0:
  9.9 98.2 all-gather.1
where the time goes:
time: 489 us; the launch traced here: 479 us
  waiting for transfers between devices  209 us (43%)
  blocking collectives  146 us (30%)
  local copies, waits for them, and re-layouts  66.1 us (14%)
  matrix products  23.3 us (5%)
  between operations  15.3 us (3%)
  other arithmetic  11.2 us (2%)
  starting transfers between devices  8.94 us (2%)
    all_to_all x1, blocking collectives, shards(): lax.all_to_all(outgoing, 'expert', split_axis=0, concat_axis=0, tiled=True)  146 us
    all_to_all x1, waiting for transfers between devices, shards(): lax.all_to_all(output_rows, 'expert', split_axis=0, concat_axis=0, tiled=...  141 us
    all_gather x1, waiting for transfers between devices, shards(): lax.all_gather(o_rows, 'expert', axis=0, tiled=True)  67.1 us
    gather x8, local copies, waits for them, and re-layouts, shards(): picked = returned_rows[flat_slot[:, route_k]].astype(jnp.float32)  47 us
  transfers between devices with their start and end apart: 4, of which 2 were waited for; matrix products, arithmetic and copies ran while one was open for 6% of the time, Pallas kernels for 0%

commit v1 on v0

v1 whole, which is shorter than its diff:
```python
import math

import jax
import jax.numpy as jnp
from jax import lax
from jax.experimental import pallas as pl
from jax.experimental.pallas import tpu as pltpu
from jax.sharding import PartitionSpec as P

MESH = pl.DeviceIdType.MESH
HEADS = 16
HD = 128
D = 2048
FF = 512
TOPK = 8
SPAN = 128
NX, NY, NZ = 4, 4, 8
WIDE = D + 128
F32 = jnp.float32
BF16 = jnp.bfloat16
REL = (2, 1, 3, 0)


def seq(i):
    return (2 + 3 * i + 3 * (i // 2) + 2 * (i // 3)) % 4


def layer_kernel(
    q_hbm, span_hbm, cache_hbm, resid_hbm, o_hbm, win_hbm, wout_hbm,
    len_ref, routes_ref, wts_ref, gain_ref,
    out_ref,
    q, kk, vv, resid, plen, bias, att, obuf, proj, proj_in, res,
    wi, wo, xbuf, qbuf, hid, r1, r2, r3, r4,
    loc, pk_s, pk_r, sc_s, sc_r, oz_s, oz_r, o2_s, o2_r, o3_s, o3_r, at_s, at_r,
    pr_s, pr_r, w_s, w_r, g1_s, g1_r, g2_s, g2_r, g3_s, g3_r, g4_s, g4_r, gp_s, gp_r,
    q_s, q_r, r1_s, r1_r, r2_s, r2_r, r3_s, r3_r, r4_s, r4_r,
):
    g = lax.axis_index("group")
    e = lax.axis_index("expert")
    x, c = g // 2, g % 2
    y, z = e // NZ, e % NZ
    oc = 1 - c

    def dev(x_=x, c_=c, y_=y, z_=z):
        return (x_ * 2 + c_, y_ * NZ + z_)

    partner = dev(c_=oc)
    twin = (z, y * NZ + g)

    def rc(src, dst, ss, rs, to):
        return pltpu.make_async_remote_copy(
            src_ref=src, dst_ref=dst, send_sem=ss, recv_sem=rs, device_id=to, device_id_type=MESH
        )

    sent = []

    def send(src, dst, ss, rs, to, keep=None):
        copy = rc(src, dst, ss, rs, to)
        copy.start()
        (sent if keep is None else keep).append(copy)

    def landed(dst, ss, rs):
        rc(dst, dst, ss, rs, partner).wait_recv()

    loads = [
        pltpu.make_async_copy(q_hbm, q, loc.at[0]),
        pltpu.make_async_copy(span_hbm.at[0], kk.at[pl.ds(0, 128)], loc.at[1]),
        pltpu.make_async_copy(span_hbm.at[1], vv.at[pl.ds(0, 128)], loc.at[2]),
        pltpu.make_async_copy(cache_hbm.at[0, 0, 0], kk.at[pl.ds(128, 128)], loc.at[3]),
        pltpu.make_async_copy(cache_hbm.at[1, 0, 0], vv.at[pl.ds(128, 128)], loc.at[4]),
        pltpu.make_async_copy(resid_hbm, resid, loc.at[5]),
    ]
    for load in loads:
        load.start()
    half_cols = pl.ds(pl.multiple_of(c * 1024, 128), 1024)
    other_cols = pl.ds(pl.multiple_of(oc * 1024, 128), 1024)
    my16 = pl.ds(pl.multiple_of(x * 16, 16), 16)
    own_o = pltpu.make_async_copy(o_hbm.at[my16, half_cols], obuf.at[y, z, my16], loc.at[6])
    own_o.start()

    barrier = pltpu.get_barrier_semaphore()
    greet = [partner]
    greet += [dev(x_=(x + d) % NX) for d in range(1, NX)]
    greet += [dev(y_=(y + d) % NY) for d in range(1, NY)]
    greet += [dev(z_=(z + d) % NZ) for d in range(1, NZ)]
    for peer in greet:
        pl.semaphore_signal(barrier, inc=1, device_id=peer, device_id_type=MESH)

    @pl.when(z != g)
    def _():
        pl.semaphore_signal(barrier, inc=1, device_id=twin, device_id_type=MESH)
        pl.semaphore_wait(barrier, len(greet) + 1)

    @pl.when(z == g)
    def _():
        pl.semaphore_wait(barrier, len(greet))

    send(cache_hbm.at[0, 0, 1], kk.at[pl.ds(256, 128)], pk_s.at[0], pk_r.at[0], partner)
    send(cache_hbm.at[1, 0, 1], vv.at[pl.ds(256, 128)], pk_s.at[1], pk_r.at[1], partner)
    send(len_ref.at[1], plen, pk_s.at[2], pk_r.at[2], partner)

    for d in range(1, NZ):
        send(
            o_hbm.at[my16, half_cols], obuf.at[y, z, my16],
            oz_s.at[d - 1], oz_r.at[d - 1], dev(z_=(z + d) % NZ),
        )

    src_i = pl.ds(pl.multiple_of(g * 256, 256), 256)
    src_o = pl.ds(pl.multiple_of(g * 64, 64), 64)
    dst_i = pl.ds(pl.multiple_of(z * 256, 256), 256)
    dst_o = pl.ds(pl.multiple_of(z * 64, 64), 64)
    twin_copies = (
        rc(win_hbm.at[0, src_i], wi.at[src_i], sc_s.at[0], sc_r.at[0], twin),
        rc(wout_hbm.at[0, src_o], wo.at[src_o], sc_s.at[1], sc_r.at[1], twin),
    )
    self_copies = (
        pltpu.make_async_copy(win_hbm.at[0, dst_i], wi.at[dst_i], sc_r.at[0]),
        pltpu.make_async_copy(wout_hbm.at[0, dst_o], wo.at[dst_o], sc_r.at[1]),
    )

    @pl.when(z != g)
    def _():
        for copy in twin_copies:
            copy.start()

    @pl.when(z == g)
    def _():
        for copy in self_copies:
            copy.start()

    def twin_wait():
        @pl.when(z != g)
        def _():
            landed(wi.at[dst_i], sc_s.at[0], sc_r.at[0])
            landed(wo.at[dst_o], sc_s.at[1], sc_r.at[1])

        @pl.when(z == g)
        def _():
            for copy in self_copies:
                copy.wait()

    def part(way, owner):
        rows_i = pl.ds(pl.multiple_of(owner * 256 + way * 128, 128), 128)
        rows_o = pl.ds(pl.multiple_of(owner * 64 + way * 32, 32), 32)
        return wi.at[rows_i], wo.at[rows_o]

    def ring_send(step):
        for way, sign in ((0, 1), (1, -1)):
            owner = (z - sign * (step - 1) + NZ) % NZ
            to = dev(z_=(z + sign + NZ) % NZ)
            for k, ref in enumerate(part(way, owner)):
                send(ref, ref, w_s.at[way, step - 1, k], w_r.at[way, step - 1, k], to)

    def ring_wait(step):
        for way, sign in ((0, 1), (1, -1)):
            owner = (z - sign * step + NZ) % NZ
            for k, ref in enumerate(part(way, owner)):
                landed(ref, w_s.at[way, step - 1, k], w_r.at[way, step - 1, k])

    def ring(step):
        ring_wait(step)
        if step < NZ - 1:
            ring_send(step + 1)

    def o_stage2():
        own_o.wait()
        for d in range(1, NZ):
            ref = obuf.at[y, (z - d + NZ) % NZ, my16]
            landed(ref, oz_s.at[d - 1], oz_r.at[d - 1])
        for u in range(2):
            ref = obuf.at[y, :, my16, pl.ds(512 * u, 512)]
            for d in range(1, 4):
                to = dev(x_=(x + d) % NX) if u == 0 else dev(y_=(y + d) % NY)
                send(ref, ref, o2_s.at[u, d - 1], o2_r.at[u, d - 1], to)

    def o_stage3():
        for u in range(2):
            for d in range(1, 4):
                if u == 0:
                    from16 = pl.ds(pl.multiple_of((x - d + NX) % NX * 16, 16), 16)
                    ref = obuf.at[y, :, from16, pl.ds(0, 512)]
                else:
                    ref = obuf.at[(y - d + NY) % NY, :, my16, pl.ds(512, 512)]
                landed(ref, o2_s.at[u, d - 1], o2_r.at[u, d - 1])
        for u in range(2):
            for d in range(1, 4):
                if u == 0:
                    ref, to = obuf.at[y, :, :, pl.ds(0, 512)], dev(y_=(y + d) % NY)
                else:
                    ref, to = obuf.at[:, :, my16, pl.ds(512, 512)], dev(x_=(x + d) % NX)
                send(ref, ref, o3_s.at[u, d - 1], o3_r.at[u, d - 1], to)

    def o_finish():
        for u in range(2):
            for d in range(1, 4):
                if u == 0:
                    ref = obuf.at[(y - d + NY) % NY, :, :, pl.ds(0, 512)]
                else:
                    from16 = pl.ds(pl.multiple_of((x - d + NX) % NX * 16, 16), 16)
                    ref = obuf.at[:, :, from16, pl.ds(512, 512)]
                landed(ref, o3_s.at[u, d - 1], o3_r.at[u, d - 1])

    for load in loads:
        load.wait()
    o_stage2()
    landed(kk.at[pl.ds(256, 128)], pk_s.at[0], pk_r.at[0])
    landed(vv.at[pl.ds(256, 128)], pk_s.at[1], pk_r.at[1])
    landed(plen, pk_s.at[2], pk_r.at[2])
    lane = lax.broadcasted_iota(jnp.int32, (8, 128), 1)
    bias[:, 0:128] = jnp.zeros((8, 128), F32)
    bias[:, 128:256] = jnp.where(lane < len_ref[0], 0.0, -1e30)
    bias[:, 256:384] = jnp.where(lane < plen[...], 0.0, -1e30)

    def heads(i):
        for j in range(2):
            cols = pl.ds(pl.multiple_of(i * 256 + j * 128, 128), 128)
            s = lax.dot_general(
                q[:, cols], kk[:, cols], (((1,), (1,)), ((), ())), preferred_element_type=F32
            )
            s = s * (1.0 / math.sqrt(HD)) + bias[0:1, :]
            m = jnp.max(s, axis=-1, keepdims=True)
            p = jnp.exp(s - m)
            total = jnp.sum(p, axis=-1, keepdims=True)
            a = jnp.dot(p.astype(BF16), vv[:, cols], preferred_element_type=F32)
            att[c, :, cols] = (a / total).astype(BF16)

    def head_range(low, high):
        @pl.loop(low, high)
        def _(i):
            heads(i)

    head_range(0, 4)
    o_stage3()
    head_range(4, 8)
    send(att.at[c], att.at[c], at_s.at[0], at_r.at[0], partner)
    twin_wait()
    ring_send(1)

    lanes = lax.broadcasted_iota(jnp.int32, (SPAN, 128), 1)
    gate_all = jnp.zeros((SPAN, 128), F32)
    for k in range(TOPK):
        gate_all += jnp.where(lanes == routes_ref[:, k:k + 1], wts_ref[:, k:k + 1], 0.0)
    xbuf[c, x, y, :, D:] = gate_all.astype(BF16)

    landed(att.at[oc], at_s.at[0], at_r.at[0])
    o_finish()
    both = 2 * SPAN

    @pl.loop(0, 2)
    def _(t):
        cols = pl.ds(pl.multiple_of(t * 512, 512), 512)
        proj[:, :, cols] = jnp.dot(
            att[...].reshape(both, D), obuf[:, :, :, cols].reshape(D, 512),
            preferred_element_type=F32,
        ).reshape(2, SPAN, 512)

    send(proj.at[oc], proj_in, pr_s.at[0], pr_r.at[0], partner)
    res[:, half_cols] = resid[:, half_cols].astype(F32) + proj[c]
    landed(proj_in, pr_s.at[0], pr_r.at[0])
    res[:, other_cols] = resid[:, other_cols].astype(F32) + proj_in[...]

    @pl.loop(0, 4)
    def _(t):
        rows = pl.ds(pl.multiple_of(t * 32, 32), 32)
        r = res[rows, :]
        scale = lax.rsqrt(jnp.mean(r * r, axis=-1, keepdims=True) + 1e-05)
        xbuf[c, x, y, rows, 0:D] = (r * scale * gain_ref[...]).astype(BF16)

    gathers = []

    def axis_of(hf, first):
        return (x, y)[hf ^ (not first)]

    def xy(hf, o, p):
        return (o, p) if hf == 0 else (p, o)

    def step(hf, on_o, d):
        if (hf == 0) == on_o:
            return dev(x_=(x + d) % 4)
        return dev(y_=(y + d) % 4)

    def mine(hf):
        return (x, y) if hf == 0 else (y, x)

    def piece(hf, j, k, low=0, size=64):
        o, p = mine(hf)
        xx, yy = xy(hf, (o + j) % 4, (p + k) % 4)
        return xbuf.at[c, xx, yy, pl.ds(64 * hf + low, size)]

    def gather_send(hf, j, k, low, size, on_o, d, ss, rs):
        ref = piece(hf, j, k, low, size)
        send(ref, ref, ss, rs, step(hf, on_o, d), gathers)

    def to_partner(hf, j, k):
        ref = piece(hf, j, k)
        send(ref, ref, gp_s.at[hf, j, k], gp_r.at[hf, j, k], partner, gathers)

    def first_over(hf):
        for w, d in ((0, 1), (1, 3)):
            gather_send(hf, 0, 0, 0, 64, True, d, g1_s.at[hf, w], g1_r.at[hf, w])

    def then_over(hf, j):
        for w, d in ((0, 1), (1, 3)):
            gather_send(hf, j, 0, 0, 64, False, d, g3_s.at[hf, j, w], g3_r.at[hf, j, w])
        to_partner(hf, j, 0)

    def first_pass(hf):
        for w, d in ((0, 1), (1, 3)):
            landed(piece(hf, 4 - d, 0), g1_s.at[hf, w], g1_r.at[hf, w])
            gather_send(hf, 4 - d, 0, 32 * w, 32, True, d, g2_s.at[hf, w], g2_r.at[hf, w])
        for d in (1, 3):
            then_over(hf, 4 - d)

    def first_end(hf):
        for w in range(2):
            landed(piece(hf, 2, 0, 32 * w, 32), g2_s.at[hf, w], g2_r.at[hf, w])
        then_over(hf, 2)

    def then_pass(hf, j):
        for w, d in ((0, 1), (1, 3)):
            landed(piece(hf, j, 4 - d), g3_s.at[hf, j, w], g3_r.at[hf, j, w])
            gather_send(hf, j, 4 - d, 32 * w, 32, False, d, g4_s.at[hf, j, w], g4_r.at[hf, j, w])
        for d in (1, 3):
            to_partner(hf, j, 4 - d)

    def then_end(hf, j):
        for w in range(2):
            landed(piece(hf, j, 2, 32 * w, 32), g4_s.at[hf, j, w], g4_r.at[hf, j, w])
        to_partner(hf, j, 2)

    for hf in range(2):
        first_over(hf)
    for hf in range(2):
        then_over(hf, 0)
    ring(1)
    for hf in range(2):
        first_pass(hf)
    for hf in range(2):
        then_pass(hf, 0)
    ring(2)
    for hf in range(2):
        first_end(hf)
    for j in (1, 3):
        for hf in range(2):
            then_pass(hf, j)
        ring(3 if j == 1 else 4)
    for hf in range(2):
        then_pass(hf, 2)
    ring(5)
    for j in (0, 1, 3, 2):
        for hf in range(2):
            then_end(hf, j)
        if j == 1:
            ring(6)
    for hf in range(2):
        o, p = mine(hf)
        for j in range(4):
            for k in range(4):
                xx, yy = xy(hf, (o + j) % 4, (p + k) % 4)
                landed(xbuf.at[oc, xx, yy, pl.ds(64 * hf, 64)], gp_s.at[hf, j, k], gp_r.at[hf, j, k])
    for copy in gathers:
        copy.wait_send()
    ring(7)

    me = y * NZ + g

    def result_copy(xx, yy):
        return rc(
            xbuf.at[oc, xx, yy, :, pl.ds(0, D)], qbuf.at[xx, yy],
            q_s.at[xx * 4 + yy], q_r.at[xx * 4 + yy], partner,
        )

    def expert_block(xx, yy):
        @pl.loop(0, 2)
        def _(t):
            left = pl.ds(pl.multiple_of(t * 256, 256), 256)
            right = pl.ds(pl.multiple_of(t * 256 + 512, 256), 256)
            rows = xbuf[:, xx, yy, :, 0:D].reshape(both, D)
            gate = jnp.dot(rows, wi[:, left], preferred_element_type=F32)
            up = jnp.dot(rows, wi[:, right], preferred_element_type=F32)
            hid[:, left] = (jax.nn.silu(gate) * up).astype(BF16)

        gates = xbuf[:, xx, yy, :, D:].reshape(both, 128).astype(F32)
        pick = lax.broadcasted_iota(jnp.int32, (both, 128), 1) == me
        weight = jnp.sum(jnp.where(pick, gates, 0.0), axis=-1, keepdims=True)

        @pl.loop(0, 4)
        def _(t):
            cols = pl.ds(pl.multiple_of(t * 512, 512), 512)
            part_out = jnp.dot(hid[...], wo[:, cols], preferred_element_type=F32) * weight
            xbuf[:, xx, yy, :, cols] = part_out.astype(BF16).reshape(2, SPAN, 512)

        result_copy(xx, yy).start()

    def add_partner(xx, yy):
        landed(qbuf.at[xx, yy], q_s.at[xx * 4 + yy], q_r.at[xx * 4 + yy])

        @pl.loop(0, 4)
        def _(t):
            rows = pl.ds(pl.multiple_of(t * 32, 32), 32)
            total = xbuf[c, xx, yy, rows, 0:D].astype(F32) + qbuf[xx, yy, rows].astype(F32)
            xbuf[c, xx, yy, rows, 0:D] = total.astype(BF16)

    def run(blocks, body):
        count, place = blocks

        @pl.loop(0, count)
        def _(i):
            dx, dy = place(i)
            body((x + dx) % 4, (y + dy) % 4)

    batches = (
        (4, lambda i: (seq(i), 2)),
        (3, lambda i: (2, seq(i + 1))),
        (3, lambda i: (1, seq(i + 1))),
        (3, lambda i: (3, seq(i + 1))),
        (3, lambda i: (0, seq(i + 1))),
    )

    def sums(hf, j, k, low=0, size=64):
        o, p = mine(hf)
        xx, yy = xy(hf, (o + j) % 4, (p + k) % 4)
        return xbuf.at[c, xx, yy, pl.ds(64 * hf + low, size), pl.ds(0, D)]

    def add_into(target, *terms):
        total = target[...].astype(F32)
        for term in terms:
            total += term[...].astype(F32)
        target[...] = total.astype(BF16)

    def back1(hf, j):
        for w, d in ((0, 1), (1, 3)):
            send(
                sums(hf, j, 2, 32 * w, 32), r1.at[hf, w, j],
                r1_s.at[hf, w, j], r1_r.at[hf, w, j], step(hf, False, d),
            )

    def back2(hf, j):
        for w, d in ((0, 1), (1, 3)):
            landed(r1.at[hf, w, j], r1_s.at[hf, w, j], r1_r.at[hf, w, j])
            add_into(sums(hf, j, d, 32 * w, 32), r1.at[hf, w, j])
        for w, d in ((0, 1), (1, 3)):
            send(
                sums(hf, j, d), r2.at[hf, w, j],
                r2_s.at[hf, w, j], r2_r.at[hf, w, j], step(hf, False, d),
            )

    def back3(hf, j):
        for w in range(2):
            landed(r2.at[hf, w, j], r2_s.at[hf, w, j], r2_r.at[hf, w, j])
        add_into(sums(hf, j, 0), r2.at[hf, 0, j], r2.at[hf, 1, j])

    def home1(hf):
        for w, d in ((0, 1), (1, 3)):
            send(
                sums(hf, 2, 0, 32 * w, 32), r3.at[hf, w],
                r3_s.at[hf, w], r3_r.at[hf, w], step(hf, True, d),
            )

    def home2(hf):
        for w, d in ((0, 1), (1, 3)):
            landed(r3.at[hf, w], r3_s.at[hf, w], r3_r.at[hf, w])
            add_into(sums(hf, d, 0, 32 * w, 32), r3.at[hf, w])
        for w, d in ((0, 1), (1, 3)):
            send(
                sums(hf, d, 0), r4.at[hf, w],
                r4_s.at[hf, w], r4_r.at[hf, w], step(hf, True, d),
            )

    def home3(hf):
        for w in range(2):
            landed(r4.at[hf, w], r4_s.at[hf, w], r4_r.at[hf, w])
        rows = pl.ds(64 * hf, 64)
        total = sums(hf, 0, 0)[...].astype(F32) + r4[hf, 0].astype(F32) + r4[hf, 1].astype(F32)
        out_ref[rows, :] = (res[rows, :] + total).astype(BF16)

    run(batches[0], expert_block)
    run(batches[1], expert_block)
    run(batches[0], add_partner)
    for j in REL:
        back1(0, j)
    run(batches[2], expert_block)
    run(batches[1], add_partner)
    for j in REL:
        back1(1, j)
    back2(0, 2)
    run(batches[3], expert_block)
    run(batches[2], add_partner)
    back2(0, 1)
    run(batches[4], expert_block)
    run(batches[3], add_partner)
    back2(1, 2)
    back2(0, 3)
    back2(1, 1)
    back2(1, 3)
    back2(1, 0)
    run(batches[4], add_partner)
    back2(0, 0)
    for hf in range(2):
        back3(hf, 2)
        home1(hf)
    for hf in range(2):
        back3(hf, 1)
        back3(hf, 3)
        home2(hf)
    for hf in range(2):
        back3(hf, 0)
    for hf in range(2):
        home3(hf)

    @pl.when(z != g)
    def _():
        for copy in twin_copies:
            copy.wait_send()

    @pl.loop(0, 16)
    def _(i):
        result_copy(i // 4, i % 4).wait_send()

    for copy in sent:
        copy.wait_send()


def shards(
    resid, queries, span_kv, cache_kv, seg_len, o_rows, norm_gain, routes, route_wts, w_in, w_out
):
    lens = jnp.broadcast_to(seg_len[0][:, None, None], (2, 8, 128))
    dma = pltpu.SemaphoreType.DMA
    vmem = pltpu.VMEM
    hbm = pl.BlockSpec(memory_space=pl.ANY)
    local = pl.BlockSpec(memory_space=pltpu.VMEM)
    return pl.pallas_call(
        layer_kernel,
        out_shape=jax.ShapeDtypeStruct((SPAN, D), BF16),
        in_specs=[hbm] * 7 + [local] * 4,
        out_specs=local,
        scratch_shapes=[
            vmem((SPAN, D), BF16),
            vmem((3 * SPAN, D), BF16),
            vmem((3 * SPAN, D), BF16),
            vmem((SPAN, D), BF16),
            vmem((8, 128), jnp.int32),
            vmem((8, 384), F32),
            vmem((2, SPAN, D), BF16),
            vmem((NY, NZ, 64, 1024), BF16),
            vmem((2, SPAN, 1024), F32),
            vmem((SPAN, 1024), F32),
            vmem((SPAN, D), F32),
            vmem((D, 2 * FF), BF16),
            vmem((FF, D), BF16),
            vmem((2, NX, NY, SPAN, WIDE), BF16),
            vmem((NX, NY, SPAN, D), BF16),
            vmem((2 * SPAN, FF), BF16),
            vmem((2, 2, 4, 32, D), BF16),
            vmem((2, 2, 4, 64, D), BF16),
            vmem((2, 2, 32, D), BF16),
            vmem((2, 2, 64, D), BF16),
            dma((7,)), dma((3,)), dma((3,)), dma((2,)), dma((2,)),
            dma((7,)), dma((7,)), dma((2, 3)), dma((2, 3)), dma((2, 3)), dma((2, 3)),
            dma((1,)), dma((1,)), dma((1,)), dma((1,)),
            dma((2, 7, 2)), dma((2, 7, 2)),
            dma((2, 2)), dma((2, 2)), dma((2, 2)), dma((2, 2)),
            dma((2, 4, 2)), dma((2, 4, 2)), dma((2, 4, 2)), dma((2, 4, 2)),
            dma((2, 4, 4)), dma((2, 4, 4)),
            dma((16,)), dma((16,)),
            dma((2, 2, 4)), dma((2, 2, 4)), dma((2, 2, 4)), dma((2, 2, 4)),
            dma((2, 2)), dma((2, 2)), dma((2, 2)), dma((2, 2)),
        ],
        compiler_params=pltpu.CompilerParams(
            collective_id=0, has_side_effects=True, vmem_limit_bytes=67043328
        ),
    )(
        queries, span_kv, cache_kv, resid, o_rows, w_in, w_out,
        lens, routes, route_wts, norm_gain.reshape(1, D),
    )


def solution(mesh):
    placed = (
        P(("group", "expert"), None),
        P(("group", "expert"), None),
        P(None, ("group", "expert"), None),
        P(None, ("group", "expert"), None, None, None),
        P(("group", "expert"), None),
        P("expert", None),
        P(),
        P(("group", "expert"), None),
        P(("group", "expert"), None),
        P("expert", None, None),
        P("expert", None, None),
    )
    return jax.shard_map(
        shards, mesh=mesh, in_specs=placed, out_specs=P(("group", "expert"), None), check_vma=False
    )
```

time: 489 us -> 253 us (0.52); the launches traced: 479 us -> 251 us
  Pallas kernels: 0 us -> 245 us
  waiting for transfers between devices: 209 us -> 0 us
  blocking collectives: 146 us -> 0 us
  local copies, waits for them, and re-layouts: 66.1 us -> 6.02 us
  matrix products: 23.3 us -> 0 us
  between operations: 15.3 us -> 0.01 us
  other arithmetic: 11.2 us -> 0 us
  starting transfers between devices: 8.94 us -> 0 us
    pallas_call x0 -> x1, Pallas kernels: none -> 245 us  [shards(): pl.pallas_call(layer_kernel, out_shape=jax.ShapeDtypeStruct((SPAN, D), BF...]
    all_to_all x1 -> x0, blocking collectives: 146 us -> none  [shards(): lax.all_to_all(outgoing, 'expert', split_axis=0, concat_axis=0, tiled=True)]
    all_to_all x1 -> x0, waiting for transfers between devices: 141 us -> none  [shards(): lax.all_to_all(output_rows, 'expert', split_axis=0, concat_axis=0, tiled=...]
    all_gather x1 -> x0, waiting for transfers between devices: 67.1 us -> none  [shards(): lax.all_gather(o_rows, 'expert', axis=0, tiled=True)]
    gather x8 -> x0, local copies, waits for them, and re-layouts: 47 us -> none  [shards(): picked = returned_rows[flat_slot[:, route_k]].astype(jnp.float32)]
    dot_general x8 -> x0, matrix products: 23.3 us -> none  [the longest x1 6.82 us: expert_mlp(): joined = jnp.dot(token_rows, weight_in, preferred_element_type=jnp.float32)]
    slice x7 -> x0, local copies, waits for them, and re-layouts: 11.5 us -> none  [the longest x4 7.51 us: shards(): vals_a = jnp.concatenate([span_kv[1], cache_kv[1, 0, 0]], axis=0)]
    all_to_all x1 -> x0, starting transfers between devices: 7.35 us -> none  [shards(): lax.all_to_all(output_rows, 'expert', split_axis=0, concat_axis=0, tiled=...]
  transfers between devices with their start and end apart: 4 -> 0, of which waited for: 2 -> 0; matrix products, arithmetic and copies ran while one was open for 6% -> 0% of each run, Pallas kernels for 0% -> 0%
where the time goes in v1:
time: 253 us; the launch traced here: 251 us
  Pallas kernels  245 us (97%)
  local copies, waits for them, and re-layouts  6.02 us (2%)
    pallas_call x1, Pallas kernels, shards(): pl.pallas_call(layer_kernel, out_shape=jax.ShapeDtypeStruct((SPAN, D), BF...  245 us

profile of v1, /device:TPU:33, one launch (start us, length us, event | category | flops | bytes accessed | tf_op | source)
XLA Modules:
  0.0 250.7 jit_solution(16299190854579620504)
XLA Ops:
  0.0 1.3 broadcast_in_dim.8.len_ref
  1.3 1.4 copy.12.routes_ref
  2.7 1.4 copy.13.wts_ref
  4.1 244.6 %shard_map.109 = bf16[128,2048]{1,0:T(8,128)(2,1)} custom-call(bf16[128,2048]{1,0:T(8,128)(2,1)} %q_hbm.1, bf16[2,128,2048]{2,1,0:T(8,128)(2,1)} %span_hbm.1, bf16[2,1,2,128,2048]{4,3,2,1,0:T(8,128)(2,1)} %cache_hbm.1, bf16[128,2048]{1,0:T(8,128)(2,1)} %resid_hbm.1, bf16[64,2048]{1,0:T(8,128)(2,1)} %o_hbm.1, bf16[1,2048,1024]{2,1,0:T(8,128)(2,1)} %win_hbm.1, ...), custom_call_target="tpu_custom_call" | custom-call | tf_op jit(solution)/shard_map/pallas_call | solution.py:532
  248.8 1.9 copy.15
